TPU v7x, 128 devices: a whole 4x4x4 slice. The times are simulated.
128 devices in a mesh: layer: 8 (over z_hi, x), feat: 16 (over z_lo, y, core).
Axes of the slice: x: 4, y: 4, z: 4 (z_hi: 2, z_lo: 2; z = z_hi * 2 + z_lo), core: 2. Of those that a mesh axis runs over, the one named last changes fastest.
Arguments:
- activations: bfloat16 [4, 1024, 32768], P(None, None, ('layer', 'feat')), may hold values from -6 to 6
- active_blocks: int32 [4, 1024, 256], P(None, None, ('layer', 'feat')), may hold values from 0 to 1, as said below
- cotangent: bfloat16 [4, 1024, 2048], P(None, 'layer', 'feat'), may hold values from -6 to 6
- decoder: bfloat16 [10, 32768, 2048], P(None, ('layer', 'feat')), may hold values from -0.03125 to 0.03125
Outputs:
- decoder_grad: bfloat16 [10, 32768, 2048], P(None, ('layer', 'feat'))
- feature_grad: bfloat16 [4, 1024, 32768], P(None, None, ('layer', 'feat'))
Inputs may be any that keep to these rules, and one draw needn't show every extreme that they name: `active_blocks`: 1 where the block of 128 features is active for that token at that layer, else 0.
All inputs are finite; a program needn't handle non-finite values.
Results may differ from a plain program's by a relative error of at most 0.001.
Values may be sent and summed in bfloat16 or wider, within the bound.
A program may use at most 128 MiB of HBM per device.

v0:
```python
import jax
import jax.numpy as jnp
from jax import lax
from jax.sharding import PartitionSpec as P


def pair_work(sparse, upstream, weights, layers):
    grads = []
    partial_value = jnp.zeros((layers, sparse.shape[1], sparse.shape[2]), jnp.float32)
    offset = 0
    for target in range(layers):
        count = target + 1
        rows = weights[offset : offset + count]
        grads.append(
            jnp.einsum(
                "stf,td->sfd", sparse[:count], upstream[target], preferred_element_type=jnp.float32
            )
        )
        terms = jnp.einsum(
            "td,sfd->stf", upstream[target], rows, preferred_element_type=jnp.float32
        )
        partial_value = partial_value.at[:count].add(terms)
        offset = offset + count
    return (jnp.concatenate(grads, axis=0), partial_value)


def body(activations, active_blocks, cotangent, decoder):
    width = activations.shape[2] // active_blocks.shape[2]
    layers = activations.shape[0]
    feature_mask = jnp.repeat(active_blocks, width, axis=2).astype(jnp.float32)
    sparse = (activations.astype(jnp.float32) * feature_mask).astype(jnp.bfloat16)
    cot_rows = lax.all_gather(cotangent, "layer", axis=1, tiled=True)
    upstream = lax.all_gather(cot_rows, "feat", axis=2, tiled=True)
    weight_grads, partial_value = pair_work(sparse, upstream, decoder, layers)
    feature_grad = (partial_value * feature_mask).astype(jnp.bfloat16)
    return (weight_grads.astype(jnp.bfloat16), feature_grad)


def solution(mesh):
    in_specs = (
        P(None, None, ("layer", "feat")),
        P(None, None, ("layer", "feat")),
        P(None, "layer", "feat"),
        P(None, ("layer", "feat"), None),
    )
    out_specs = (P(None, ("layer", "feat"), None), P(None, None, ("layer", "feat")))
    return jax.shard_map(body, mesh=mesh, in_specs=in_specs, out_specs=out_specs, check_vma=False)
```

profile of v0, /device:TPU:1, one launch (start us, length us, event | category | flops | bytes accessed | tf_op | source)
XLA Modules:
  0.0 217.0 jit_solution(17988041659607771263)
XLA Ops:
  7.2 0.0 all-gather.3.cloned.1.call-start
  7.2 0.7 all-gather.3.cloned.1.call-update
  7.9 0.0 all-gather.5.cloned.1.call-start
  7.9 51.1 %all-gather.3.cloned.1.call-done = bf16[4,1024,128]{2,1,0:T(8,128)(2,1)} async-done(((bf16[4,128,128]{2,1,0:T(8,128)(2,1)}), bf16[4,1024,128]{2,1,0:T(8,128)(2,1)}) %all-gather.3.cloned.1.call-update) | async-done | bytes 1048592 | tf_op jit(solution)/shard_map/all_gather | solution.py:32
  59.1 0.0 all-gather.5.cloned.1.call-update
  59.1 0.8 convert_element_type.18
  59.9 3.0 %copy.6 = bf16[4,1024,256]{1,2,0:T(8,128)(2,1)S(1)} copy(bf16[4,1024,256]{2,1,0:T(8,128)(2,1)} %param.14) | data formatting | bytes 4194304 | tf_op args[0]
  62.9 1.9 fusion
  64.8 94.6 %all-gather.5.cloned.1.call-done = bf16[4,1024,2048]{2,1,0:T(8,128)(2,1)} async-done(((bf16[4,1024,128]{2,1,0:T(8,128)(2,1)}), bf16[4,1024,2048]{2,1,0:T(8,128)(2,1)}) %all-gather.5.cloned.1.call-update) | async-done | bytes 16777232 | tf_op jit(solution)/shard_map/all_gather | solution.py:33
  159.4 3.8 %fusion.15 = f32[1,1024,256]{1,2,0:T(8,128)S(1)} fusion(bf16[4,1024,2048]{2,1,0:T(8,128)(2,1)} %all-gather.5.cloned.1.call-done, bf16[10,256,2048]{2,1,0:T(8,128)(2,1)} %param.17), kind=kOutput, calls=%fused_computation.26 | convolution fusion | flops 1073741824 | bytes 6291456 | tf_op jit(solution)/shard_map/td,sfd->stf/dot_general | solution.py:19
  163.2 0.0 slice-start
  163.2 0.5 scatter-add.10
  163.7 0.0 slice-start.1
  163.7 0.0 slice-start.2
  163.7 5.6 %fusion.14 = f32[4,1024,256]{1,2,0:T(8,128)S(1)} fusion(f32[4,1024,256]{1,2,0:T(8,128)S(1)} %scatter-add.10, bf16[10,256,2048]{2,1,0:T(8,128)(2,1)} %param.17, bf16[4,1024,2048]{2,1,0:T(8,128)(2,1)} %all-gather.5.cloned.1.call-done), kind=kOutput, calls=%fused_computation.25 | convolution fusion | flops 2148007936 | bytes 18874368 | tf_op jit(solution)/shard_map/td,sfd->stf/dot_general | solution.py:19
  169.4 0.0 slice-done
  169.4 0.0 slice-done.1
  169.4 0.0 slice-done.2
  169.4 5.5 %fusion.10 = f32[4,1024,256]{1,2,0:T(8,128)S(1)} fusion(f32[4,1024,256]{1,2,0:T(8,128)S(1)} %fusion.14, bf16[10,256,2048]{2,1,0:T(8,128)(2,1)S(1)} %bitcast.71, bf16[4,1024,2048]{2,1,0:T(8,128)(2,1)} %all-gather.5.cloned.1.call-done), kind=kOutput, calls=%fused_computation.20 | convolution fusion | flops 3222011904 | bytes 20971520 | tf_op jit(solution)/shard_map/td,sfd->stf/dot_general | solution.py:19
  174.9 7.0 %fusion.1 = bf16[4,1024,256]{1,2,0:T(8,128)(2,1)S(1)} fusion(f32[4,1024,256]{1,2,0:T(8,128)S(1)} %fusion.10, f32[4,1024,2]{1,2,0:T(2,128)S(1)} %convert_element_type.18, bf16[10,256,2048]{2,1,0:T(8,128)(2,1)S(1)} %bitcast.71, bf16[4,1024,2048]{2,1,0:T(8,128)(2,1)} %all-gather.5.cloned.1.call-done), kind=kOutput, calls=%fused_computation.4 | convolution fusion | flops 4298113024 | bytes 21004288 | tf_op jit(solution)/shard_map/td,sfd->stf/dot_general | solution.py:19
  181.9 2.6 %copy.7 = bf16[4,1024,256]{2,1,0:T(8,128)(2,1)} copy(bf16[4,1024,256]{1,2,0:T(8,128)(2,1)S(1)} %fusion.1) | data formatting | bytes 4194304
  184.4 7.5 %convolution_convert_fusion = bf16[4,256,2048]{2,1,0:T(8,128)(2,1)S(1)} fusion(bf16[4,1024,256]{1,2,0:T(8,128)(2,1)} %fusion, bf16[4,1024,2048]{2,1,0:T(8,128)(2,1)} %all-gather.5.cloned.1.call-done), kind=kOutput, calls=%fused_computation.10 | convolution fusion | flops 4297064448 | bytes 10485760 | tf_op jit(solution)/shard_map/stf,td->sfd/dot_general | solution.py:15
  191.9 0.0 copy-done
  191.9 0.0 slice-start.6
  191.9 6.2 %fusion.9 = bf16[3,256,2048]{2,1,0:T(8,128)(2,1)S(1)} fusion(bf16[4,1024,256]{1,2,0:T(8,128)(2,1)S(1)} %copy-done, bf16[4,1024,2048]{2,1,0:T(8,128)(2,1)} %all-gather.5.cloned.1.call-done), kind=kOutput, calls=%fused_computation.18 | convolution fusion | flops 3222798336 | bytes 9437184 | tf_op jit(solution)/shard_map/stf,td->sfd/dot_general | solution.py:15
  198.1 0.0 slice-done.3
  198.1 0.0 slice-done.4
  198.1 0.0 slice-done.5
  198.1 0.0 slice-done.6
  198.1 2.4 %fusion.11 = bf16[2,256,2048]{2,1,0:T(8,128)(2,1)S(1)} fusion(bf16[4,1024,256]{1,2,0:T(8,128)(2,1)S(1)} %copy-done, bf16[4,1024,2048]{2,1,0:T(8,128)(2,1)S(1)} %bitcast.73), kind=kOutput, calls=%fused_computation.21 | convolution fusion | flops 2148532224 | bytes 8388608 | tf_op jit(solution)/shard_map/stf,td->sfd/dot_general | solution.py:15
  200.5 1.3 fusion.13
  201.8 8.4 %pad_maximum_fusion = bf16[10,256,2048]{2,1,0:T(8,128)(2,1)} fusion(bf16[4,256,2048]{2,1,0:T(8,128)(2,1)S(1)} %convolution_convert_fusion, bf16[3,256,2048]{2,1,0:T(8,128)(2,1)S(1)} %fusion.9, bf16[2,256,2048]{2,1,0:T(8,128)(2,1)S(1)} %fusion.11, bf16[1,256,2048]{2,1,0:T(8,128)(2,1)S(1)} %fusion.13), kind=kLoop, calls=%fused_computation | loop fusion | flops 15728640 | bytes 20971520 | tf_op jit(solution)/shard_map/concatenate | solution.py:24
  (6 shorter events, 0.0 us)
Async XLA Ops:
  7.2 51.9 %all-gather.3.cloned.1.call-start = ((), (), s32[]{:S(2)}) async-start(), calls=%async_computation | async-start | bytes 1179648 | tf_op jit(solution)/shard_map/all_gather | solution.py:32
  7.9 151.5 %all-gather.5.cloned.1.call-start = ((), (), s32[]{:S(2)}) async-start(), calls=%async_computation.1 | async-start | bytes 17825792 | tf_op jit(solution)/shard_map/all_gather | solution.py:33
  163.2 6.2 %slice-start = ((s8[10485760]{0:T(1024)(128)(4,1)}), s8[4194304]{0:T(1024)(128)(4,1)S(1)}, s32[]{:S(2)}) async-start(s8[10485760]{0:T(1024)(128)(4,1)} %bitcast.70), calls=%async_computation.2 | async-start | bytes 8388608
  163.7 5.7 %slice-start.1 = ((s8[10485760]{0:T(1024)(128)(4,1)}), s8[4194304]{0:T(1024)(128)(4,1)S(1)}, s32[]{:S(2)}) async-start(s8[10485760]{0:T(1024)(128)(4,1)} %bitcast.70), calls=%async_computation.3 | async-start | bytes 8388608
  163.7 5.7 %slice-start.2 = ((s8[10485760]{0:T(1024)(128)(4,1)}), s8[2097152]{0:T(1024)(128)(4,1)S(1)}, s32[]{:S(2)}) async-start(s8[10485760]{0:T(1024)(128)(4,1)} %bitcast.70), calls=%async_computation.4 | async-start | bytes 4194304
  184.4 7.5 %copy-start = (bf16[4,1024,256]{1,2,0:T(8,128)(2,1)S(1)}, bf16[4,1024,256]{1,2,0:T(8,128)(2,1)}, u32[]{:S(2)}) copy-start(bf16[4,1024,256]{1,2,0:T(8,128)(2,1)} %fusion) | copy-start | bytes 6291460
  184.4 13.7 %slice-start.3 = ((s8[16777216]{0:T(1024)(128)(4,1)}), s8[4194304]{0:T(1024)(128)(4,1)S(1)}, s32[]{:S(2)}) async-start(s8[16777216]{0:T(1024)(128)(4,1)} %bitcast.72), calls=%async_computation.5 | async-start | bytes 8388608
  184.4 13.7 %slice-start.4 = ((s8[16777216]{0:T(1024)(128)(4,1)}), s8[4194304]{0:T(1024)(128)(4,1)S(1)}, s32[]{:S(2)}) async-start(s8[16777216]{0:T(1024)(128)(4,1)} %bitcast.72), calls=%async_computation.6 | async-start | bytes 8388608
  184.4 13.7 %slice-start.5 = ((s8[16777216]{0:T(1024)(128)(4,1)}), s8[4194304]{0:T(1024)(128)(4,1)S(1)}, s32[]{:S(2)}) async-start(s8[16777216]{0:T(1024)(128)(4,1)} %bitcast.72), calls=%async_computation.7 | async-start | bytes 8388608
  191.9 6.2 %slice-start.6 = ((s8[16777216]{0:T(1024)(128)(4,1)}), s8[4194304]{0:T(1024)(128)(4,1)S(1)}, s32[]{:S(2)}) async-start(s8[16777216]{0:T(1024)(128)(4,1)} %bitcast.72), calls=%async_computation.8 | async-start | bytes 8388608
Sparse Core Ops, SparseCore 0:
  10.3 48.6 all-gather.2
  60.7 98.6 all-gather.4
where the time goes:
time: 217 us
  waiting for transfers between devices  146 us (67%)
  matrix products  39.1 us (18%)
  between operations  14.2 us (7%)
  other arithmetic  11 us (5%)
  local copies, waits for them, and re-layouts  6.11 us (3%)
    all_gather x1, waiting for transfers between devices, body(): upstream = lax.all_gather(cot_rows, 'feat', axis=2, tiled=True)  94.6 us
    all_gather x1, waiting for transfers between devices, body(): cot_rows = lax.all_gather(cotangent, 'layer', axis=1, tiled=True)  51.1 us
    dot_general x4, matrix products, pair_work(): jnp.einsum('td,sfd->stf', upstream[target], rows, preferred_element_type=...  21.9 us
    dot_general x4, matrix products, pair_work(): jnp.einsum('stf,td->sfd', sparse[:count], upstream[target], preferred_ele...  17.3 us
    concatenate x1, other arithmetic, pair_work(): return (jnp.concatenate(grads, axis=0), partial_value)  8.37 us
    unnamed x18, local copies, waits for them, and re-layouts  5.6 us
  transfers between devices with their start and end apart: 2, of which 2 were waited for; matrix products, arithmetic and copies ran while one was open for 3% of the time, Pallas kernels for 0%

commit v1 on v0

--- a/solution.py
+++ b/solution.py
@@ -30,7 +30,9 @@
     feature_mask = jnp.repeat(active_blocks, width, axis=2).astype(jnp.float32)
     sparse = (activations.astype(jnp.float32) * feature_mask).astype(jnp.bfloat16)
     cot_rows = lax.all_gather(cotangent, "layer", axis=1, tiled=True)
-    upstream = lax.all_gather(cot_rows, "feat", axis=2, tiled=True)
+    upstream = jnp.concatenate(
+        lax.all_to_all(jnp.stack([cot_rows] * lax.axis_size("feat")), "feat", 0, 0), axis=2
+    )
     weight_grads, partial_value = pair_work(sparse, upstream, decoder, layers)
     feature_grad = (partial_value * feature_mask).astype(jnp.bfloat16)
     return (weight_grads.astype(jnp.bfloat16), feature_grad)

time: 217 us -> 380 us (1.75)
  waiting for transfers between devices: 146 us -> 271 us
  local copies, waits for them, and re-layouts: 6.11 us -> 44.7 us
  matrix products: 39.1 us -> 30.7 us
  starting transfers between devices: 0.08 us -> 7.3 us
    all_to_all x0 -> x1, waiting for transfers between devices: none -> 219 us  [body(): lax.all_to_all(jnp.stack([cot_rows] * lax.axis_size('feat')), 'feat', 0, 0)]
    all_gather x1 -> x0, waiting for transfers between devices: 94.6 us -> none  [body(): upstream = lax.all_gather(cot_rows, 'feat', axis=2, tiled=True)]
    all_to_all x0 -> x1, local copies, waits for them, and re-layouts: none -> 22.6 us  [body(): lax.all_to_all(jnp.stack([cot_rows] * lax.axis_size('feat')), 'feat', 0, 0)]
    slice x0 -> x1, local copies, waits for them, and re-layouts: none -> 8.91 us  [pair_work(): upstream[target]]
    dot_general x4, matrix products: 21.9 us -> 13.6 us  [pair_work(): jnp.einsum('td,sfd->stf', upstream[target], rows, preferred_element_type=...]
    all_to_all x0 -> x1, starting transfers between devices: none -> 7.26 us  [body(): lax.all_to_all(jnp.stack([cot_rows] * lax.axis_size('feat')), 'feat', 0, 0)]
    another operation x0 -> x1, local copies, waits for them, and re-layouts: none -> 7.03 us  [body(): jnp.stack([cot_rows] * lax.axis_size('feat'))]
  transfers between devices with their start and end apart: 2 -> 2, of which waited for: 2 -> 2; matrix products, arithmetic and copies ran while one was open for 3% -> 1% of each run, Pallas kernels for 0% -> 0%
where the time goes in v1:
time: 380 us; the launch traced here: 379 us
  waiting for transfers between devices  271 us (71%)
  local copies, waits for them, and re-layouts  44.7 us (12%)
  matrix products  30.7 us (8%)
  between operations  14.2 us (4%)
  other arithmetic  10.9 us (3%)
  starting transfers between devices  7.3 us (2%)
    all_to_all x1, waiting for transfers between devices, body(): lax.all_to_all(jnp.stack([cot_rows] * lax.axis_size('feat')), 'feat', 0, 0)  219 us
    all_gather x1, waiting for transfers between devices, body(): cot_rows = lax.all_gather(cotangent, 'layer', axis=1, tiled=True)  51.2 us
    all_to_all x1, local copies, waits for them, and re-layouts, body(): lax.all_to_all(jnp.stack([cot_rows] * lax.axis_size('feat')), 'feat', 0, 0)  22.6 us
    dot_general x4, matrix products, pair_work(): jnp.einsum('stf,td->sfd', sparse[:count], upstream[target], preferred_ele...  17.1 us
    dot_general x4, matrix products, pair_work(): jnp.einsum('td,sfd->stf', upstream[target], rows, preferred_element_type=...  13.6 us
    concatenate x1, other arithmetic, pair_work(): return (jnp.concatenate(grads, axis=0), partial_value)  9.03 us
    slice x1, local copies, waits for them, and re-layouts, pair_work(): upstream[target]  8.91 us
  transfers between devices with their start and end apart: 2, of which 2 were waited for; matrix products, arithmetic and copies ran while one was open for 1% of the time, Pallas kernels for 0%

profile of v1, /device:TPU:1, one launch (start us, length us, event | category | flops | bytes accessed | tf_op | source)
XLA Modules:
  0.0 378.8 jit_solution(17059909106581690044)
XLA Ops:
  7.2 0.0 all-gather.2.cloned.1.call-start
  7.2 0.7 all-gather.2.cloned.1.call-update
  7.9 51.2 %all-gather.2.cloned.1.call-done = bf16[4,1024,128]{2,1,0:T(8,128)(2,1)} async-done(((bf16[4,128,128]{2,1,0:T(8,128)(2,1)}), bf16[4,1024,128]{2,1,0:T(8,128)(2,1)}) %all-gather.2.cloned.1.call-update) | async-done | bytes 1048592 | tf_op jit(solution)/shard_map/all_gather | solution.py:32
  59.1 7.0 %stack.2 = bf16[16,4,1024,128]{3,2,1,0:T(8,128)(2,1)} broadcast(bf16[4,1024,128]{2,1,0:T(8,128)(2,1)} %all-gather.2.cloned.1.call-done), dimensions={1,2,3} | broadcast | bytes 17825792 | tf_op jit(solution)/shard_map/stack | solution.py:34
  66.1 0.0 copy-start.4
  66.1 7.3 %all-to-all-start = ((bf16[16,4,1024,128]{3,2,1,0:T(8,128)(2,1)}), bf16[16,4,1024,128]{3,2,1,0:T(8,128)(2,1)}, u32[]{:S(2)}, u32[]{:S(2)}) async-start(bf16[16,4,1024,128]{3,2,1,0:T(8,128)(2,1)} %stack.2), calls=%async_computation | async-start | bytes 33554432 | tf_op jit(solution)/shard_map/all_to_all | solution.py:34
  73.4 0.0 copy-done.4
  73.4 3.0 copy.13
  76.4 1.9 fusion
  78.3 219.3 %all-to-all-done = bf16[16,4,1024,128]{3,2,1,0:T(8,128)(2,1)} async-done(((bf16[16,4,1024,128]{3,2,1,0:T(8,128)(2,1)}), bf16[16,4,1024,128]{3,2,1,0:T(8,128)(2,1)}, u32[]{:S(2)}, u32[]{:S(2)}) %all-to-all-start) | async-done | bytes 16777248 | tf_op jit(solution)/shard_map/all_to_all | solution.py:34
  297.5 22.6 %copy.14 = bf16[16,4,1024,128]{2,3,0,1:T(8,128)(2,1)} copy(bf16[16,4,1024,128]{3,2,1,0:T(8,128)(2,1)} %all-to-all-done) | data formatting | bytes 33554432 | tf_op jit(solution)/shard_map/all_to_all | solution.py:34
  320.2 8.9 %fusion.7 = (bf16[1,1024,16,128]{1,3,2,0:T(8,128)(2,1)S(1)}, bf16[1,1024,16,128]{1,3,2,0:T(8,128)(2,1)S(1)}, bf16[1,1024,16,128]{1,3,2,0:T(8,128)(2,1)S(1)}, bf16[1,1024,16,128]{1,3,2,0:T(8,128)(2,1)}) fusion(bf16[4,1024,16,128]{1,3,2,0:T(8,128)(2,1)} %bitcast.60), kind=kLoop, calls=%fused_computation.19 | loop fusion | bytes 33554432 | tf_op jit(solution)/shard_map/slice | solution.py:16
  329.1 2.7 convolution_bitcast_fusion
  331.8 0.0 copy-done.1
  331.8 0.0 slice-start
  331.8 2.3 fusion.3
  334.0 0.0 copy-done
  334.1 3.8 %convolution_convert_fusion.2 = bf16[2,256,2048]{2,1,0:T(8,128)(2,1)} fusion(bf16[4,1024,256]{1,2,0:T(8,128)(2,1)S(1)} %copy-done.1, bf16[1024,2048,1]{0,1,2:T(8,128)(2,1)S(1)} %bitcast.67), kind=kOutput, calls=%fused_computation.10 | convolution fusion | flops 2148532224 | bytes 8388608 | tf_op jit(solution)/shard_map/stf,td->sfd/dot_general | solution.py:15
  337.9 0.5 scatter-add.10
  338.4 0.0 slice-done
  338.4 0.0 slice-done.1
  338.4 0.0 slice-done.2
  338.4 2.5 fusion.4
  340.9 4.9 %convolution_convert_fusion.1 = bf16[3,256,2048]{2,1,0:T(8,128)(2,1)} fusion(bf16[4,1024,256]{1,2,0:T(8,128)(2,1)S(1)} %copy-done.1, bf16[1024,2048,1]{0,1,2:T(8,128)(2,1)S(1)} %bitcast.65), kind=kOutput, calls=%fused_computation.7 | convolution fusion | flops 3222798336 | bytes 9437184 | tf_op jit(solution)/shard_map/stf,td->sfd/dot_general | solution.py:15
  345.8 3.7 fusion.2
  349.5 0.0 copy-done.2
  349.5 6.1 %convolution_convert_fusion = bf16[4,256,2048]{2,1,0:T(8,128)(2,1)} fusion(bf16[4,1024,256]{1,2,0:T(8,128)(2,1)S(1)} %copy-done.2, bf16[1024,2048,1]{0,1,2:T(8,128)(2,1)S(1)} %bitcast.61), kind=kOutput, calls=%fused_computation.6 | convolution fusion | flops 4297064448 | bytes 10485760 | tf_op jit(solution)/shard_map/stf,td->sfd/dot_general | solution.py:15
  355.6 4.7 %fusion.1 = bf16[4,1024,256]{1,2,0:T(8,128)(2,1)S(1)} fusion(f32[4,1024,256]{1,2,0:T(8,128)S(1)} %fusion.2, bf16[10,256,2048]{2,1,0:T(8,128)(2,1)S(1)} %bitcast.64, bf16[1024,2048,1]{0,1,2:T(8,128)(2,1)S(1)} %bitcast.62, f32[4,1024,2]{1,2,0:T(2,128)S(1)} %convert_element_type.18), kind=kOutput, calls=%fused_computation.4 | convolution fusion | flops 4298113024 | bytes 21004288 | tf_op jit(solution)/shard_map/td,sfd->stf/dot_general | solution.py:19
  360.4 0.0 copy-start.3
  360.4 2.6 copy.18
  362.9 0.0 copy-done.3
  363.0 9.0 %pad_maximum_fusion = bf16[10,256,2048]{2,1,0:T(8,128)(2,1)} fusion(bf16[4,256,2048]{2,1,0:T(8,128)(2,1)} %convolution_convert_fusion, bf16[3,256,2048]{2,1,0:T(8,128)(2,1)} %convolution_convert_fusion.1, bf16[2,256,2048]{2,1,0:T(8,128)(2,1)} %convolution_convert_fusion.2, bf16[1,256,2048]{2,1,0:T(8,128)(2,1)S(1)} %copy-done.3), kind=kLoop, calls=%fused_computation | loop fusion | flops 15728640 | bytes 20971520 | tf_op jit(solution)/shard_map/concatenate | solution.py:24
  (7 shorter events, 0.0 us)
Async XLA Ops:
  7.2 51.9 %all-gather.2.cloned.1.call-start = ((), (), s32[]{:S(2)}) async-start(), calls=%async_computation.1 | async-start | bytes 1179648 | tf_op jit(solution)/shard_map/all_gather | solution.py:32
  66.1 7.3 %copy-start.4 = (s32[4,1024,2]{1,2,0:T(2,128)S(1)}, s32[4,1024,2]{1,2,0:T(2,128)}, u32[]{:S(2)}) copy-start(s32[4,1024,2]{1,2,0:T(2,128)} %param.15) | copy-start | bytes 98308
  66.1 231.5 %all-to-all-start = ((bf16[16,4,1024,128]{3,2,1,0:T(8,128)(2,1)}), bf16[16,4,1024,128]{3,2,1,0:T(8,128)(2,1)}, u32[]{:S(2)}, u32[]{:S(2)}) async-start(bf16[16,4,1024,128]{3,2,1,0:T(8,128)(2,1)} %stack.2), calls=%async_computation | async-start | bytes 33554432 | tf_op jit(solution)/shard_map/all_to_all | solution.py:34
  329.1 2.7 copy-start.1
  329.1 5.0 %copy-start = (bf16[1,1024,16,128]{1,3,2,0:T(8,128)(2,1)S(1)}, bf16[1,1024,16,128]{1,3,2,0:T(8,128)(2,1)}, u32[]{:S(2)}) copy-start(bf16[1,1024,16,128]{1,3,2,0:T(8,128)(2,1)} %get-tuple-element.67) | copy-start | bytes 12582916
  331.8 6.6 %slice-start = ((s8[10485760]{0:T(1024)(128)(4,1)}), s8[4194304]{0:T(1024)(128)(4,1)S(1)}, s32[]{:S(2)}) async-start(s8[10485760]{0:T(1024)(128)(4,1)} %bitcast.63), calls=%async_computation.2 | async-start | bytes 8388608
  334.1 4.3 %slice-start.1 = ((s8[10485760]{0:T(1024)(128)(4,1)}), s8[4194304]{0:T(1024)(128)(4,1)S(1)}, s32[]{:S(2)}) async-start(s8[10485760]{0:T(1024)(128)(4,1)} %bitcast.63), calls=%async_computation.3 | async-start | bytes 8388608
  334.1 4.3 %slice-start.2 = ((s8[10485760]{0:T(1024)(128)(4,1)}), s8[2097152]{0:T(1024)(128)(4,1)S(1)}, s32[]{:S(2)}) async-start(s8[10485760]{0:T(1024)(128)(4,1)} %bitcast.63), calls=%async_computation.4 | async-start | bytes 4194304
  345.8 3.7 copy-start.2
  360.4 2.6 copy-start.3
Sparse Core Ops, SparseCore 0:
  10.3 48.6 all-gather.1
